TPU v7x, 32 devices: a whole 2x2x4 slice. The times are simulated.
32 devices in a mesh: gx: 4 (over z), gy: 8 (over y, x, core).
Axes of the slice: x: 2, y: 2, z: 4, core: 2. Of those that a mesh axis runs over, the one named last changes fastest.
Arguments:
- rock_props: float32 [4, 4, 128, 768], P(None, None, 'gx', 'gy'), may hold values from 0.1 to 10
- block_slot: int32 [128, 768], P('gx', 'gy'), may hold values from 0 to 11, as said below
- bases_start: float32 [12, 4, 256, 1024], P(None, None, 'gx', 'gy'), may hold values from 0.1 to 1
Outputs:
- bases: float32 [12, 4, 256, 1024], P(None, None, 'gx', 'gy')
Inputs may be any that keep to these rules, and one draw needn't show every extreme that they name: `block_slot`: within one tile the numbers used are 0 up to some count minus one, each constant on aligned 16 x 16 squares and never falling in row-major order of the squares; the tile at the grid's corner uses all 12.
All inputs are finite; a program needn't handle non-finite values.
Results may differ from a plain program's by a relative error of at most 0.0003.
Values sent between devices are 32-bit elements; how exact they have to be, the bound alone decides.
A program may use at most 64 MiB of HBM per device.

v0:
```python
import jax
import jax.numpy as jnp
from jax import lax
from jax.sharding import PartitionSpec as P

MARGIN = 16
ITERS = 2
SWEEPS = 3
NB = 12


relax_weight = 2.0 / 3.0


def extended(block, sides, width):
    for axis, dim in sides:
        count = lax.axis_size(axis)
        forward = [(i, i + 1) for i in range(count - 1)]
        backward = [(target, source) for source, target in forward]
        low = lax.ppermute(
            lax.slice_in_dim(block, block.shape[dim] - width, None, axis=dim), axis, forward
        )
        high = lax.ppermute(lax.slice_in_dim(block, 0, width, axis=dim), axis, backward)
        block = jnp.concatenate([low, block, high], axis=dim)
    return block


def harmonic(first_k, second_k):
    return 2.0 * first_k * second_k / jnp.maximum(first_k + second_k, 0.1)


def coefficients(perm_x, perm_y, perm_z, storage):
    trans_x = harmonic(perm_x[..., :-1, 1:-1], perm_x[..., 1:, 1:-1])
    trans_y = harmonic(perm_y[..., 1:-1, :-1], perm_y[..., 1:-1, 1:])
    inner_z = perm_z[..., 1:-1, 1:-1]
    trans_z = harmonic(inner_z[..., :-1, :, :], inner_z[..., 1:, :, :])
    zero_layer = jnp.zeros_like(inner_z[..., :1, :, :])
    below = jnp.concatenate([zero_layer, trans_z], axis=-3)
    above = jnp.concatenate([trans_z, zero_layer], axis=-3)
    links = (
        trans_x[..., :-1, :],
        trans_x[..., 1:, :],
        trans_y[..., :-1],
        trans_y[..., 1:],
        below,
        above,
    )
    total = links[0] + links[1] + links[2] + links[3] + links[4] + links[5]
    diagonal = jnp.maximum(total + 0.05 * storage[..., 1:-1, 1:-1], 0.01)
    return (links, diagonal)


def jacobi_sweep(current, links, diagonal, support):
    width = [(0, 0)] * (current.ndim - 3) + [(1, 1)] * 3
    padded = jnp.pad(current, width)
    neighbour = (
        links[0] * padded[..., 1:-1, :-2, 1:-1]
        + links[1] * padded[..., 1:-1, 2:, 1:-1]
        + links[2] * padded[..., 1:-1, 1:-1, :-2]
        + links[3] * padded[..., 1:-1, 1:-1, 2:]
        + links[4] * padded[..., :-2, 1:-1, 1:-1]
        + links[5] * padded[..., 2:, 1:-1, 1:-1]
    )
    return support * ((1.0 - relax_weight) * current + relax_weight * neighbour / diagonal)


def dilate(own_cells):
    span = 2 * MARGIN + 1
    window_dims = (1,) * (own_cells.ndim - 2) + (span, span)
    return lax.reduce_window(
        own_cells,
        jnp.array(0.0, own_cells.dtype),
        lax.max,
        window_dims,
        (1,) * own_cells.ndim,
        "SAME",
    )


def totals(partial_value):
    margin = MARGIN
    rows_here = partial_value.shape[1] - 2 * margin
    cols_here = partial_value.shape[2] - 2 * margin
    strips = jnp.concatenate([partial_value[:, : 2 * margin], partial_value[:, rows_here:]], axis=1)
    received = extended(strips, (("gx", 1),), 2 * margin)
    partial_value = partial_value.at[:, : 2 * margin].add(received[:, : 2 * margin])
    partial_value = partial_value.at[:, rows_here:].add(received[:, 6 * margin :])
    strips = jnp.concatenate(
        [partial_value[..., : 2 * margin], partial_value[..., cols_here:]], axis=2
    )
    received = extended(strips, (("gy", 2),), 2 * margin)
    partial_value = partial_value.at[..., : 2 * margin].add(received[..., : 2 * margin])
    partial_value = partial_value.at[..., cols_here:].add(received[..., 6 * margin :])
    return partial_value


def body(rock_props, block_slot, bases_start):
    margin = MARGIN
    rock_window = extended(rock_props, (("gx", 2), ("gy", 3)), margin + 1)
    links, diagonal = coefficients(rock_window[0], rock_window[1], rock_window[2], rock_window[3])
    inside = (rock_window[0, 0, 1:-1, 1:-1] > 0.0).astype(rock_props.dtype)
    slot_ids = jnp.arange(NB, dtype=jnp.int32)
    own_cells = (block_slot[None] == slot_ids[:, None, None]).astype(rock_props.dtype)
    own_cells = jnp.pad(own_cells, ((0, 0), (margin, margin), (margin, margin)))
    support = (dilate(own_cells) * inside)[:, None]
    bases_now = support * (own_cells[:, None] + bases_start)
    for turn in range(ITERS):
        for sweep_no in range(SWEEPS):
            bases_now = jacobi_sweep(bases_now, links, diagonal, support)
        partial_value = jnp.sum(bases_now, axis=0)
        sums = totals(partial_value)
        bases_now = bases_now / jnp.maximum(sums, 0.01)
    return bases_now


def solution(mesh):
    placed = (P(None, None, "gx", "gy"), P("gx", "gy"), P(None, None, "gx", "gy"))
    return jax.shard_map(
        body, mesh=mesh, in_specs=placed, out_specs=P(None, None, "gx", "gy"), check_vma=False
    )
```

profile of v0, /device:TPU:11, one launch (start us, length us, event | category | flops | bytes accessed | tf_op | source)
XLA Modules:
  0.0 133.8 jit_solution(14104399700483326123)
XLA Ops:
  1.1 3.2 %collective-permute-start = (f32[4,4,17,96]{3,2,1,0:T(8,128)S(1)}, f32[4,4,17,96]{3,2,1,0:T(8,128)S(1)}, u32[]{:S(2)}, u32[]{:S(2)}) collective-permute-start(f32[4,4,17,96]{3,2,1,0:T(8,128)S(1)} %get-tuple-element.114), channel_id=1, source_target_pairs={{0,8},{8,16},{16,24},{1,9},{9,17},{17,25},{2,10},{10,18},{18,26},{... | collective-permute-start | bytes 313352 | tf_op jit(solution)/shard_map/ppermute | solution.py:20
  4.3 2.1 %collective-permute-start.1 = (f32[4,4,17,96]{3,2,1,0:T(8,128)S(1)}, f32[4,4,17,96]{3,2,1,0:T(8,128)S(1)}, u32[]{:S(2)}, u32[]{:S(2)}) collective-permute-start(f32[4,4,17,96]{3,2,1,0:T(8,128)S(1)} %get-tuple-element.115), channel_id=1, source_target_pairs={{8,0},{16,8},{24,16},{9,1},{17,9},{25,17},{10,2},{18,10},{26,18},{... | collective-permute-start | bytes 313352 | tf_op jit(solution)/shard_map/ppermute | solution.py:23
  6.4 2.4 %collective-permute-done = f32[4,4,17,96]{3,2,1,0:T(8,128)S(1)} collective-permute-done((f32[4,4,17,96]{3,2,1,0:T(8,128)S(1)}, f32[4,4,17,96]{3,2,1,0:T(8,128)S(1)}, u32[]{:S(2)}, u32[]{:S(2)}) %collective-permute-start) | collective-permute-done | bytes 104480 | tf_op jit(solution)/shard_map/ppermute | solution.py:20
  8.7 2.9 %collective-permute-done.1 = f32[4,4,17,96]{3,2,1,0:T(8,128)S(1)} collective-permute-done((f32[4,4,17,96]{3,2,1,0:T(8,128)S(1)}, f32[4,4,17,96]{3,2,1,0:T(8,128)S(1)}, u32[]{:S(2)}, u32[]{:S(2)}) %collective-permute-start.1) | collective-permute-done | bytes 104480 | tf_op jit(solution)/shard_map/ppermute | solution.py:23
  13.5 3.7 %collective-permute-start.3 = (f32[4,4,66,17]{2,3,1,0:T(8,128)S(1)}, f32[4,4,66,17]{2,3,1,0:T(8,128)S(1)}, u32[]{:S(2)}, u32[]{:S(2)}) collective-permute-start(f32[4,4,66,17]{2,3,1,0:T(8,128)S(1)} %copy.22), channel_id=1, source_target_pairs={{1,0},{2,1},{3,2},{4,3},{5,4},{6,5},{7,6},{9,8},{10,9},{11,10},{12... | collective-permute-start | bytes 215432 | tf_op jit(solution)/shard_map/ppermute | solution.py:23
  17.2 3.0 %collective-permute-start.2 = (f32[4,4,66,17]{2,3,1,0:T(8,128)S(1)}, f32[4,4,66,17]{2,3,1,0:T(8,128)S(1)}, u32[]{:S(2)}, u32[]{:S(2)}) collective-permute-start(f32[4,4,66,17]{2,3,1,0:T(8,128)S(1)} %copy.21), channel_id=1, source_target_pairs={{0,1},{1,2},{2,3},{3,4},{4,5},{5,6},{6,7},{8,9},{9,10},{10,11},{11... | collective-permute-start | bytes 215432 | tf_op jit(solution)/shard_map/ppermute | solution.py:20
  20.4 47.4 %reduce_window.7 = f32[12,64,128]{2,0,1:T(8,128)S(1)} reduce-window(f32[12,32,96]{2,0,1:T(8,128)S(1)} %fusion.90, f32[]{:T(128)} %constant.200.clone.1), window={size=1x33x33 pad=0_0x32_32x32_32}, to_apply=%region_0.1 | reduce-window | flops 106954752 | bytes 540676 | tf_op jit(solution)/shard_map/reduce_window | solution.py:70
  74.4 1.6 %fusion.97 = (f32[4,64,128]{2,1,0:T(8,128)S(1)}, f32[12,4,64,128]{3,2,1,0:T(8,128)S(1)}) fusion(f32[4,64,128]{2,1,0:T(8,128)S(1)} %get-tuple-element.112, f32[4,64,128]{2,1,0:T(8,128)S(1)} %get-tuple-element.127, f32[4,64,128]{2,1,0:T(8,128)S(1)} %get-tuple-element.126, f32[4,64,128]{2,1,0:T(8,128)S(1)} %get-tuple-element.113, ...), kind=kLoop, calls=%fused_computation.159 | loop fusion | flops 6651904 | bytes 4587520 | tf_op jit(solution)/shard_map/reduce_sum | solution.py:110
  76.0 3.2 %collective-permute-start.4 = (f32[4,32,128]{2,1,0:T(8,128)S(1)}, f32[4,32,128]{2,1,0:T(8,128)S(1)}, u32[]{:S(2)}, u32[]{:S(2)}) collective-permute-start(f32[4,32,128]{2,1,0:T(8,128)S(1)} %slice.465), channel_id=1, source_target_pairs={{0,8},{8,16},{16,24},{1,9},{9,17},{17,25},{2,10},{10,18},{18,26},{... | collective-permute-start | bytes 196616 | tf_op jit(solution)/shard_map/ppermute | solution.py:20
  79.2 2.5 %collective-permute-done.4 = f32[4,32,128]{2,1,0:T(8,128)S(1)} collective-permute-done((f32[4,32,128]{2,1,0:T(8,128)S(1)}, f32[4,32,128]{2,1,0:T(8,128)S(1)}, u32[]{:S(2)}, u32[]{:S(2)}) %collective-permute-start.4) | collective-permute-done | bytes 65568 | tf_op jit(solution)/shard_map/ppermute | solution.py:20
  81.8 1.9 %collective-permute-start.5 = (f32[4,32,128]{2,1,0:T(8,128)S(1)}, f32[4,32,128]{2,1,0:T(8,128)S(1)}, u32[]{:S(2)}, u32[]{:S(2)}) collective-permute-start(f32[4,32,128]{2,1,0:T(8,128)S(1)} %get-tuple-element.124), channel_id=1, source_target_pairs={{8,0},{16,8},{24,16},{9,1},{17,9},{25,17},{10,2},{18,10},{26,18},{... | collective-permute-start | bytes 196616 | tf_op jit(solution)/shard_map/ppermute | solution.py:23
  83.7 3.1 %collective-permute-done.5 = f32[4,32,128]{2,1,0:T(8,128)S(1)} collective-permute-done((f32[4,32,128]{2,1,0:T(8,128)S(1)}, f32[4,32,128]{2,1,0:T(8,128)S(1)}, u32[]{:S(2)}, u32[]{:S(2)}) %collective-permute-start.5) | collective-permute-done | bytes 65568 | tf_op jit(solution)/shard_map/ppermute | solution.py:23
  86.9 4.5 %collective-permute-start.6 = (f32[4,64,32]{2,1,0:T(8,128)S(1)}, f32[4,64,32]{2,1,0:T(8,128)S(1)}, u32[]{:S(2)}, u32[]{:S(2)}) collective-permute-start(f32[4,64,32]{2,1,0:T(8,128)S(1)} %slice.468), channel_id=1, source_target_pairs={{0,1},{1,2},{2,3},{3,4},{4,5},{5,6},{6,7},{8,9},{9,10},{10,11},{11... | collective-permute-start | bytes 98312 | tf_op jit(solution)/shard_map/ppermute | solution.py:20
  91.5 1.9 %collective-permute-done.6 = f32[4,64,32]{2,1,0:T(8,128)S(1)} collective-permute-done((f32[4,64,32]{2,1,0:T(8,128)S(1)}, f32[4,64,32]{2,1,0:T(8,128)S(1)}, u32[]{:S(2)}, u32[]{:S(2)}) %collective-permute-start.6) | collective-permute-done | bytes 32800 | tf_op jit(solution)/shard_map/ppermute | solution.py:20
  93.4 3.4 %collective-permute-start.7 = (f32[4,64,32]{2,1,0:T(8,128)S(1)}, f32[4,64,32]{2,1,0:T(8,128)S(1)}, u32[]{:S(2)}, u32[]{:S(2)}) collective-permute-start(f32[4,64,32]{2,1,0:T(8,128)S(1)} %get-tuple-element.122), channel_id=1, source_target_pairs={{1,0},{2,1},{3,2},{4,3},{5,4},{6,5},{7,6},{9,8},{10,9},{11,10},{12... | collective-permute-start | bytes 98312 | tf_op jit(solution)/shard_map/ppermute | solution.py:23
  97.2 4.1 %collective-permute-done.7 = f32[4,64,32]{2,1,0:T(8,128)S(1)} collective-permute-done((f32[4,64,32]{2,1,0:T(8,128)S(1)}, f32[4,64,32]{2,1,0:T(8,128)S(1)}, u32[]{:S(2)}, u32[]{:S(2)}) %collective-permute-start.7) | collective-permute-done | bytes 32800 | tf_op jit(solution)/shard_map/ppermute | solution.py:23
  107.2 3.2 %collective-permute-start.8 = (f32[4,32,128]{2,1,0:T(8,128)S(1)}, f32[4,32,128]{2,1,0:T(8,128)S(1)}, u32[]{:S(2)}, u32[]{:S(2)}) collective-permute-start(f32[4,32,128]{2,1,0:T(8,128)S(1)} %slice.471), channel_id=1, source_target_pairs={{0,8},{8,16},{16,24},{1,9},{9,17},{17,25},{2,10},{10,18},{18,26},{... | collective-permute-start | bytes 196616 | tf_op jit(solution)/shard_map/ppermute | solution.py:20
  110.4 1.8 %collective-permute-done.8 = f32[4,32,128]{2,1,0:T(8,128)S(1)} collective-permute-done((f32[4,32,128]{2,1,0:T(8,128)S(1)}, f32[4,32,128]{2,1,0:T(8,128)S(1)}, u32[]{:S(2)}, u32[]{:S(2)}) %collective-permute-start.8) | collective-permute-done | bytes 65568 | tf_op jit(solution)/shard_map/ppermute | solution.py:20
  112.3 1.9 %collective-permute-start.9 = (f32[4,32,128]{2,1,0:T(8,128)S(1)}, f32[4,32,128]{2,1,0:T(8,128)S(1)}, u32[]{:S(2)}, u32[]{:S(2)}) collective-permute-start(f32[4,32,128]{2,1,0:T(8,128)S(1)} %get-tuple-element.120), channel_id=1, source_target_pairs={{8,0},{16,8},{24,16},{9,1},{17,9},{25,17},{10,2},{18,10},{26,18},{... | collective-permute-start | bytes 196616 | tf_op jit(solution)/shard_map/ppermute | solution.py:23
  114.2 3.3 %collective-permute-done.9 = f32[4,32,128]{2,1,0:T(8,128)S(1)} collective-permute-done((f32[4,32,128]{2,1,0:T(8,128)S(1)}, f32[4,32,128]{2,1,0:T(8,128)S(1)}, u32[]{:S(2)}, u32[]{:S(2)}) %collective-permute-start.9) | collective-permute-done | bytes 65568 | tf_op jit(solution)/shard_map/ppermute | solution.py:23
  117.6 3.9 %collective-permute-start.10 = (f32[4,64,32]{2,1,0:T(8,128)S(1)}, f32[4,64,32]{2,1,0:T(8,128)S(1)}, u32[]{:S(2)}, u32[]{:S(2)}) collective-permute-start(f32[4,64,32]{2,1,0:T(8,128)S(1)} %slice.474), channel_id=1, source_target_pairs={{0,1},{1,2},{2,3},{3,4},{4,5},{5,6},{6,7},{8,9},{9,10},{10,11},{11... | collective-permute-start | bytes 98312 | tf_op jit(solution)/shard_map/ppermute | solution.py:20
  121.5 1.9 %collective-permute-done.10 = f32[4,64,32]{2,1,0:T(8,128)S(1)} collective-permute-done((f32[4,64,32]{2,1,0:T(8,128)S(1)}, f32[4,64,32]{2,1,0:T(8,128)S(1)}, u32[]{:S(2)}, u32[]{:S(2)}) %collective-permute-start.10) | collective-permute-done | bytes 32800 | tf_op jit(solution)/shard_map/ppermute | solution.py:20
  123.4 2.5 %collective-permute-start.11 = (f32[4,64,32]{2,1,0:T(8,128)S(1)}, f32[4,64,32]{2,1,0:T(8,128)S(1)}, u32[]{:S(2)}, u32[]{:S(2)}) collective-permute-start(f32[4,64,32]{2,1,0:T(8,128)S(1)} %get-tuple-element.118), channel_id=1, source_target_pairs={{1,0},{2,1},{3,2},{4,3},{5,4},{6,5},{7,6},{9,8},{10,9},{11,10},{12... | collective-permute-start | bytes 98312 | tf_op jit(solution)/shard_map/ppermute | solution.py:23
  126.3 5.0 %collective-permute-done.11 = f32[4,64,32]{2,1,0:T(8,128)S(1)} collective-permute-done((f32[4,64,32]{2,1,0:T(8,128)S(1)}, f32[4,64,32]{2,1,0:T(8,128)S(1)}, u32[]{:S(2)}, u32[]{:S(2)}) %collective-permute-start.11) | collective-permute-done | bytes 32800 | tf_op jit(solution)/shard_map/ppermute | solution.py:23
  (53 shorter events, 18.8 us)
Async XLA Ops:
  1.1 7.7 %collective-permute-start = (f32[4,4,17,96]{3,2,1,0:T(8,128)S(1)}, f32[4,4,17,96]{3,2,1,0:T(8,128)S(1)}, u32[]{:S(2)}, u32[]{:S(2)}) collective-permute-start(f32[4,4,17,96]{3,2,1,0:T(8,128)S(1)} %get-tuple-element.114), channel_id=1, source_target_pairs={{0,8},{8,16},{16,24},{1,9},{9,17},{17,25},{2,10},{10,18},{18,26},{... | collective-permute-start | bytes 313352 | tf_op jit(solution)/shard_map/ppermute | solution.py:20
  4.3 7.4 %collective-permute-start.1 = (f32[4,4,17,96]{3,2,1,0:T(8,128)S(1)}, f32[4,4,17,96]{3,2,1,0:T(8,128)S(1)}, u32[]{:S(2)}, u32[]{:S(2)}) collective-permute-start(f32[4,4,17,96]{3,2,1,0:T(8,128)S(1)} %get-tuple-element.115), channel_id=1, source_target_pairs={{8,0},{16,8},{24,16},{9,1},{17,9},{25,17},{10,2},{18,10},{26,18},{... | collective-permute-start | bytes 313352 | tf_op jit(solution)/shard_map/ppermute | solution.py:23
  12.7 7.5 %copy-start.2 = (s32[32,96]{1,0:T(8,128)S(1)}, s32[32,96]{1,0:T(8,128)}, u32[]{:S(2)}) copy-start(s32[32,96]{1,0:T(8,128)} %param.20) | copy-start | bytes 36868
  13.5 54.7 %collective-permute-start.3 = (f32[4,4,66,17]{2,3,1,0:T(8,128)S(1)}, f32[4,4,66,17]{2,3,1,0:T(8,128)S(1)}, u32[]{:S(2)}, u32[]{:S(2)}) collective-permute-start(f32[4,4,66,17]{2,3,1,0:T(8,128)S(1)} %copy.22), channel_id=1, source_target_pairs={{1,0},{2,1},{3,2},{4,3},{5,4},{6,5},{7,6},{9,8},{10,9},{11,10},{12... | collective-permute-start | bytes 215432 | tf_op jit(solution)/shard_map/ppermute | solution.py:23
  17.2 50.7 %collective-permute-start.2 = (f32[4,4,66,17]{2,3,1,0:T(8,128)S(1)}, f32[4,4,66,17]{2,3,1,0:T(8,128)S(1)}, u32[]{:S(2)}, u32[]{:S(2)}) collective-permute-start(f32[4,4,66,17]{2,3,1,0:T(8,128)S(1)} %copy.21), channel_id=1, source_target_pairs={{0,1},{1,2},{2,3},{3,4},{4,5},{5,6},{6,7},{8,9},{9,10},{10,11},{11... | collective-permute-start | bytes 215432 | tf_op jit(solution)/shard_map/ppermute | solution.py:20
  20.3 48.1 %copy-start = (f32[4,4,32,96]{3,2,1,0:T(8,128)S(1)}, f32[4,4,32,96]{3,2,1,0:T(8,128)}, u32[]{:S(2)}) copy-start(f32[4,4,32,96]{3,2,1,0:T(8,128)} %param.19) | copy-start | bytes 589828
  69.5 1.4 %copy-start.1 = (f32[12,4,64,128]{3,2,1,0:T(8,128)S(1)}, f32[12,4,64,128]{3,2,1,0:T(8,128)}, u32[]{:S(2)}) copy-start(f32[12,4,64,128]{3,2,1,0:T(8,128)} %param.21) | copy-start | bytes 4718596
  76.0 5.7 %collective-permute-start.4 = (f32[4,32,128]{2,1,0:T(8,128)S(1)}, f32[4,32,128]{2,1,0:T(8,128)S(1)}, u32[]{:S(2)}, u32[]{:S(2)}) collective-permute-start(f32[4,32,128]{2,1,0:T(8,128)S(1)} %slice.465), channel_id=1, source_target_pairs={{0,8},{8,16},{16,24},{1,9},{9,17},{17,25},{2,10},{10,18},{18,26},{... | collective-permute-start | bytes 196616 | tf_op jit(solution)/shard_map/ppermute | solution.py:20
  81.8 5.0 %collective-permute-start.5 = (f32[4,32,128]{2,1,0:T(8,128)S(1)}, f32[4,32,128]{2,1,0:T(8,128)S(1)}, u32[]{:S(2)}, u32[]{:S(2)}) collective-permute-start(f32[4,32,128]{2,1,0:T(8,128)S(1)} %get-tuple-element.124), channel_id=1, source_target_pairs={{8,0},{16,8},{24,16},{9,1},{17,9},{25,17},{10,2},{18,10},{26,18},{... | collective-permute-start | bytes 196616 | tf_op jit(solution)/shard_map/ppermute | solution.py:23
  86.9 6.5 %collective-permute-start.6 = (f32[4,64,32]{2,1,0:T(8,128)S(1)}, f32[4,64,32]{2,1,0:T(8,128)S(1)}, u32[]{:S(2)}, u32[]{:S(2)}) collective-permute-start(f32[4,64,32]{2,1,0:T(8,128)S(1)} %slice.468), channel_id=1, source_target_pairs={{0,1},{1,2},{2,3},{3,4},{4,5},{5,6},{6,7},{8,9},{9,10},{10,11},{11... | collective-permute-start | bytes 98312 | tf_op jit(solution)/shard_map/ppermute | solution.py:20
  93.4 7.9 %collective-permute-start.7 = (f32[4,64,32]{2,1,0:T(8,128)S(1)}, f32[4,64,32]{2,1,0:T(8,128)S(1)}, u32[]{:S(2)}, u32[]{:S(2)}) collective-permute-start(f32[4,64,32]{2,1,0:T(8,128)S(1)} %get-tuple-element.122), channel_id=1, source_target_pairs={{1,0},{2,1},{3,2},{4,3},{5,4},{6,5},{7,6},{9,8},{10,9},{11,10},{12... | collective-permute-start | bytes 98312 | tf_op jit(solution)/shard_map/ppermute | solution.py:23
  107.2 5.0 %collective-permute-start.8 = (f32[4,32,128]{2,1,0:T(8,128)S(1)}, f32[4,32,128]{2,1,0:T(8,128)S(1)}, u32[]{:S(2)}, u32[]{:S(2)}) collective-permute-start(f32[4,32,128]{2,1,0:T(8,128)S(1)} %slice.471), channel_id=1, source_target_pairs={{0,8},{8,16},{16,24},{1,9},{9,17},{17,25},{2,10},{10,18},{18,26},{... | collective-permute-start | bytes 196616 | tf_op jit(solution)/shard_map/ppermute | solution.py:20
  112.3 5.2 %collective-permute-start.9 = (f32[4,32,128]{2,1,0:T(8,128)S(1)}, f32[4,32,128]{2,1,0:T(8,128)S(1)}, u32[]{:S(2)}, u32[]{:S(2)}) collective-permute-start(f32[4,32,128]{2,1,0:T(8,128)S(1)} %get-tuple-element.120), channel_id=1, source_target_pairs={{8,0},{16,8},{24,16},{9,1},{17,9},{25,17},{10,2},{18,10},{26,18},{... | collective-permute-start | bytes 196616 | tf_op jit(solution)/shard_map/ppermute | solution.py:23
  117.6 5.8 %collective-permute-start.10 = (f32[4,64,32]{2,1,0:T(8,128)S(1)}, f32[4,64,32]{2,1,0:T(8,128)S(1)}, u32[]{:S(2)}, u32[]{:S(2)}) collective-permute-start(f32[4,64,32]{2,1,0:T(8,128)S(1)} %slice.474), channel_id=1, source_target_pairs={{0,1},{1,2},{2,3},{3,4},{4,5},{5,6},{6,7},{8,9},{9,10},{10,11},{11... | collective-permute-start | bytes 98312 | tf_op jit(solution)/shard_map/ppermute | solution.py:20
  123.4 7.9 %collective-permute-start.11 = (f32[4,64,32]{2,1,0:T(8,128)S(1)}, f32[4,64,32]{2,1,0:T(8,128)S(1)}, u32[]{:S(2)}, u32[]{:S(2)}) collective-permute-start(f32[4,64,32]{2,1,0:T(8,128)S(1)} %get-tuple-element.118), channel_id=1, source_target_pairs={{1,0},{2,1},{3,2},{4,3},{5,4},{6,5},{7,6},{9,8},{10,9},{11,10},{12... | collective-permute-start | bytes 98312 | tf_op jit(solution)/shard_map/ppermute | solution.py:23
where the time goes:
time: 134 us
  other arithmetic  61.2 us (46%)
  starting transfers between devices  36.7 us (27%)
  waiting for transfers between devices  28.9 us (22%)
  local copies, waits for them, and re-layouts  6.54 us (5%)
    another operation x1, other arithmetic, dilate(): lax.reduce_window(own_cells, jnp.array(0.0, own_cells.dtype), lax.max, wi...  47.4 us
    ppermute x6, starting transfers between devices, extended(): lax.ppermute(lax.slice_in_dim(block, block.shape[dim] - width, None, axis...  21.1 us
    ppermute x6, waiting for transfers between devices, extended(): lax.ppermute(lax.slice_in_dim(block, 0, width, axis=dim), axis, backward)  18.4 us
    ppermute x6, starting transfers between devices, extended(): lax.ppermute(lax.slice_in_dim(block, 0, width, axis=dim), axis, backward)  15.6 us
    ppermute x6, waiting for transfers between devices, extended(): lax.ppermute(lax.slice_in_dim(block, block.shape[dim] - width, None, axis...  10.5 us
    mul x4, other arithmetic, jacobi_sweep(): support * ((1.0 - relax_weight) * current + relax_weight * neighbour / di...  5.93 us
    reduce_sum x2, other arithmetic, body(): partial_value = jnp.sum(bases_now, axis=0)  3.12 us
  transfers between devices with their start and end apart: 12, of which 10 were waited for; matrix products, arithmetic and copies ran while one was open for 36% of the time, Pallas kernels for 0%

commit v1 on v0

v1 whole, which is shorter than its diff:
```python
import functools

import jax
import jax.numpy as jnp
from jax import lax
from jax.experimental import pallas as pl
from jax.experimental.pallas import tpu as pltpu
from jax.sharding import PartitionSpec as P

MARGIN = 16
BLK = 16
ITERS = 2
SWEEPS = 3
PAD = 8
LANES = 128
COLOURS = 3
WEIGHT = 2.0 / 3.0
MESH = pl.DeviceIdType.MESH
DIRS = ((-1, -1), (1, -1), (-1, 1), (1, 1), (0, -1), (0, 1), (-1, 0), (1, 0))


def harmonic(first_k, second_k):
    return 2.0 * first_k * second_k / jnp.maximum(first_k + second_k, 0.1)


def tall(value, count):
    return jnp.concatenate([value] * count, axis=0)


def kernel(
    n_gx, n_gy,
    rock_hbm, slot_ref, start_hbm, out_hbm,
    rock, start, window, joined, strip_out, strip_in, coef, maps, span_map, packed, spanning,
    part, part_strip, part_x, part_y, part_d,
    rock_sem, start_sem, out_sem, send_sem, recv_sem,
):
    m = MARGIN
    nb, nz, ex, ey = start.shape
    tx, ty = rock.shape[2], rock.shape[3]
    rows_p = BLK + 2 * m
    full = ex + 2 * PAD
    n_win = window.shape[0]
    KX, KY, ST, TZ = 0, nz, 2 * nz, 3 * nz
    sub_y = ty // BLK
    half = ex // 2

    gx = lax.axis_index("gx")
    gy = lax.axis_index("gy")

    def exists(dx, dy):
        ok = None
        for cond in (
            [gx > 0] if dx < 0 else [gx < n_gx - 1] if dx > 0 else []
        ) + ([gy > 0] if dy < 0 else [gy < n_gy - 1] if dy > 0 else []):
            ok = cond if ok is None else jnp.logical_and(ok, cond)
        return ok

    rock_copy = pltpu.make_async_copy(rock_hbm, rock, rock_sem)
    start_copy = pltpu.make_async_copy(start_hbm, start, start_sem)
    rock_copy.start()
    start_copy.start()

    for i in range(n_win):
        window[i, : PAD + m, :] = jnp.zeros((PAD + m, ey), jnp.float32)
        window[i, PAD + m + tx :, :] = jnp.zeros((PAD + m, ey), jnp.float32)
    strip_in[...] = jnp.zeros_like(strip_in)
    part_x[...] = jnp.zeros_like(part_x)
    part_y[...] = jnp.zeros_like(part_y)
    part_d[...] = jnp.zeros_like(part_d)

    barrier = pltpu.get_barrier_semaphore()
    expected = jnp.int32(0)
    for dx, dy in DIRS:
        there = exists(dx, dy)
        expected = expected + there.astype(jnp.int32)

        @pl.when(there)
        def _(dx=dx, dy=dy):
            pl.semaphore_signal(
                barrier, inc=1, device_id=(gx + dx, gy + dy), device_id_type=MESH
            )

    def rock_messages(dx, dy):
        if dy == 0:
            if dx < 0:
                return [
                    (window.at[0:nz, pl.ds(PAD + m, m + PAD)], window.at[0:nz, pl.ds(PAD + m + tx, m + PAD)]),
                    (window.at[nz:n_win, pl.ds(PAD + m, m)], window.at[nz:n_win, pl.ds(PAD + m + tx, m)]),
                ]
            return [
                (window.at[0:nz, pl.ds(tx, m + PAD)], window.at[0:nz, pl.ds(0, m + PAD)]),
                (window.at[nz:n_win, pl.ds(PAD + tx, m)], window.at[nz:n_win, pl.ds(PAD, m)]),
            ]
        side = 0 if dy < 0 else 1
        if dx == 0:
            return [(strip_out.at[side], strip_in.at[side, :, pl.ds(PAD + m, tx)])]
        if dx < 0:
            return [(strip_out.at[side, :, pl.ds(0, m + PAD)], strip_in.at[side, :, pl.ds(PAD + m + tx, m + PAD)])]
        return [(strip_out.at[side, :, pl.ds(tx - m - PAD, m + PAD)], strip_in.at[side, :, pl.ds(0, m + PAD)])]

    def sum_messages(turn, dx, dy):
        if dy == 0:
            if dx < 0:
                return [(part.at[turn, :, pl.ds(0, half)], part_x.at[turn, :, pl.ds(half, half)])]
            return [(part.at[turn, :, pl.ds(half, half)], part_x.at[turn, :, pl.ds(0, half)])]
        side = 0 if dy < 0 else 1
        if dx == 0:
            return [(part_strip.at[turn, side], part_y.at[turn, side])]
        if dx < 0:
            return [(part_strip.at[turn, side, pl.ds(0, half)], part_d.at[turn, side, pl.ds(half, half)])]
        return [(part_strip.at[turn, side, pl.ds(half, half)], part_d.at[turn, side, pl.ds(0, half)])]

    def copies(phase, dx, dy):
        messages = rock_messages(dx, dy) if phase == 0 else sum_messages(phase - 1, dx, dy)
        base = 2 * DIRS.index((dx, dy))
        return [
            pltpu.make_async_remote_copy(
                src_ref=src,
                dst_ref=dst,
                send_sem=send_sem.at[phase, base + i],
                recv_sem=recv_sem.at[phase, base + i],
                device_id=(gx + dx, gy + dy),
                device_id_type=MESH,
            )
            for i, (src, dst) in enumerate(messages)
        ]

    def send(phase):
        for dx, dy in DIRS:
            @pl.when(exists(dx, dy))
            def _(dx=dx, dy=dy):
                for copy in copies(phase, dx, dy):
                    copy.start()

    def receive(phase):
        for dx, dy in DIRS:
            @pl.when(exists(-dx, -dy))
            def _(dx=dx, dy=dy):
                for copy in copies(phase, dx, dy):
                    copy.wait_recv()

    def sent(phase):
        for dx, dy in DIRS:
            @pl.when(exists(dx, dy))
            def _(dx=dx, dy=dy):
                for copy in copies(phase, dx, dy):
                    copy.wait_send()

    rock_copy.wait()
    lane_t = lax.broadcasted_iota(jnp.int32, (tx, ey), 1)
    own_rows = slice(PAD + m, PAD + m + tx)

    def place(i, value):
        wide = jnp.concatenate([value, jnp.zeros((tx, ey - ty), jnp.float32)], axis=1)
        window[i, own_rows, :] = pltpu.roll(wide, m, axis=1)

    for z in range(nz):
        place(KX + z, rock[0, z])
        place(KY + z, rock[1, z])
        place(ST + z, rock[3, z])
        if z < nz - 1:
            place(TZ + z, harmonic(rock[2, z], rock[2, z + 1]))
    per = LANES // m
    for side in range(2):
        first = m if side == 0 else m + ty - m
        extra = 2 * m if side == 0 else m + ty - m - 1
        for block in range(2):
            packed_strip = jnp.zeros((tx, ey), jnp.float32)
            for i in range(block * per, min(n_win, block * per + per)):
                j = i - block * per
                moved = pltpu.roll(window[i, own_rows, :], (m * j - first) % ey, axis=1)
                packed_strip = jnp.where(lane_t // m == j, moved, packed_strip)
            if block == 1:
                for z in range(nz):
                    spot = m * (per - 1) + z
                    moved = pltpu.roll(window[KY + z, own_rows, :], (spot - extra) % ey, axis=1)
                    packed_strip = jnp.where(lane_t == spot, moved, packed_strip)
            strip_out[side, block] = packed_strip

    pl.semaphore_wait(barrier, expected)
    send(0)

    lane = lax.broadcasted_iota(jnp.int32, (PAD, ey), 1)
    slot_rows = []
    for r in range(2):
        raw = slot_ref[r * BLK : r * BLK + PAD, :].astype(jnp.float32)
        wide = jnp.concatenate([raw, jnp.full((PAD, ey - ty), -9.0, jnp.float32)], axis=1)
        slot_rows.append(pltpu.roll(wide, m, axis=1))
    in_tile = jnp.logical_and(lane >= m, lane < m + ty)
    last = jnp.max(slot_rows[0], axis=1, keepdims=True)
    first = jnp.min(jnp.where(in_tile, slot_rows[1], 99.0), axis=1, keepdims=True)
    span = jnp.broadcast_to(jnp.where(last == first, last, -5.0), (PAD, ey))
    reach = []
    for r in range(2):
        near = (slot_rows[r], pltpu.roll(slot_rows[r], m, axis=1), pltpu.roll(slot_rows[r], ey - m, axis=1))
        touched = jnp.zeros((PAD, ey), jnp.float32)
        for value in near:
            touched = jnp.where(value == span, 1.0, touched)
        reach.append(touched)
        for c in range(COLOURS):
            held = jnp.full((PAD, ey), -1.0, jnp.float32)
            for value in near:
                colour = value - COLOURS * jnp.floor((value + 0.5) / COLOURS)
                fits = jnp.logical_and(value >= 0.0, jnp.logical_and(colour == float(c), value != span))
                held = jnp.where(fits, value, held)
            a = r * COLOURS + c
            maps[a, 0] = held
            taken = held >= 0.0
            low = jnp.logical_and(taken, jnp.logical_and(lane > 0, pltpu.roll(held, 1, axis=1) == held))
            high = jnp.logical_and(taken, jnp.logical_and(lane < ey - 1, pltpu.roll(held, ey - 1, axis=1) == held))
            maps[a, 1] = jnp.where(low, 1.0, 0.0)
            maps[a, 2] = jnp.where(high, 1.0, 0.0)
    both = jnp.maximum(reach[0], reach[1])
    span_map[...] = jnp.concatenate(
        [tall(reach[0], BLK // PAD), tall(both, (ex - 2 * BLK) // PAD), tall(reach[1], BLK // PAD)], axis=0
    )

    row = lax.broadcasted_iota(jnp.int32, (ex, ey), 0)
    col = lax.broadcasted_iota(jnp.int32, (ex, ey), 1)
    inside = jnp.ones((ex, ey), jnp.float32)
    edge = lambda cond: jnp.where(cond, 0.0, 1.0).astype(jnp.float32)
    inside = inside * jnp.where(row < m, edge(gx == 0), 1.0)
    inside = inside * jnp.where(row >= m + tx, edge(gx == n_gx - 1), 1.0)
    inside = inside * jnp.where(col < m, edge(gy == 0), 1.0)
    inside = inside * jnp.where(col >= m + ty, edge(gy == n_gy - 1), 1.0)

    packed[:, :, :, :PAD, :] = jnp.zeros(packed.shape[:3] + (PAD, ey), jnp.float32)
    packed[:, :, :, PAD + rows_p :, :] = jnp.zeros(packed.shape[:3] + (PAD, ey), jnp.float32)
    spanning[:, :, :PAD, :] = jnp.zeros(spanning.shape[:2] + (PAD, ey), jnp.float32)
    spanning[:, :, PAD + ex :, :] = jnp.zeros(spanning.shape[:2] + (PAD, ey), jnp.float32)
    mid = slice(PAD, PAD + rows_p)
    mid_s = slice(PAD, PAD + ex)
    n_p = rows_p // PAD
    n_s = ex // PAD
    start_copy.wait()

    def fill(z, carry):
        for r in range(2):
            rows = slice(r * BLK, r * BLK + rows_p)
            slot_count = sub_y if r == 0 else nb
            for c in range(COLOURS):
                a = r * COLOURS + c
                held = maps[a, 0]
                own = jnp.where(held == slot_rows[r], 1.0, 0.0)
                none = jnp.zeros((m, ey), jnp.float32)
                value = jnp.concatenate([none, tall(own, BLK // PAD), none], axis=0)
                held_tall = tall(held, n_p)
                for k in range(c, slot_count, COLOURS):
                    value = value + jnp.where(held_tall == float(k), start[k, z, rows, :], 0.0)
                packed[0, a, z, mid, :] = value * inside[rows]
        none = jnp.zeros((m, ey), jnp.float32)
        value = jnp.concatenate(
            [none]
            + [tall(jnp.where(slot_rows[r] == span, 1.0, 0.0), BLK // PAD) for r in range(2)]
            + [none],
            axis=0,
        )
        span_tall = tall(span, n_s)
        for k in range(sub_y):
            value = value + jnp.where(span_tall == float(k), start[k, z], 0.0)
        spanning[0, z, mid_s, :] = value * inside * span_map[...]
        return carry

    lax.fori_loop(0, nz, fill, 0)

    receive(0)
    lane_f = lax.broadcasted_iota(jnp.int32, (full, ey), 1)
    for i in range(n_win):
        block, j = i // per, i % per
        left = pltpu.roll(strip_in[1, block], (-m * j) % ey, axis=1)
        right = pltpu.roll(strip_in[0, block], (ey - m - m * j) % ey, axis=1)
        joined[i] = jnp.where(lane_f < m, left, jnp.where(lane_f >= ey - m, right, window[i]))
    lane_s = lax.broadcasted_iota(jnp.int32, (ex, ey), 1)
    for z in range(nz):
        here = joined[KX + z, mid_s, :]
        link_xl = harmonic(joined[KX + z, PAD - 1 : PAD - 1 + ex, :], here)
        link_xh = harmonic(here, joined[KX + z, PAD + 1 : PAD + 1 + ex, :])
        here = joined[KY + z, mid_s, :]
        spot = m * (per - 1) + z
        outer = pltpu.roll(strip_in[1, 1, mid_s, :], (-spot) % ey, axis=1)
        link_yl = harmonic(jnp.where(lane_s == 0, outer, pltpu.roll(here, 1, axis=1)), here)
        outer = pltpu.roll(strip_in[0, 1, mid_s, :], (ey - 1 - spot) % ey, axis=1)
        link_yh = harmonic(here, jnp.where(lane_s == ey - 1, outer, pltpu.roll(here, ey - 1, axis=1)))
        links = [link_xl, link_xh, link_yl, link_yh]
        places = [0, 1, 2, 3]
        if z > 0:
            links.append(joined[TZ + z - 1, mid_s, :])
            places.append(4)
        if z < nz - 1:
            links.append(joined[TZ + z, mid_s, :])
            places.append(5)
        total = links[0]
        for link in links[1:]:
            total = total + link
        diagonal = jnp.maximum(total + 0.05 * joined[ST + z, mid_s, :], 0.01)
        factor = WEIGHT / diagonal
        for place_no, link in zip(places, links):
            coef[place_no, z] = link * factor

    stay = 1.0 - WEIGHT

    def sweep(s, carry):
        src = lax.rem(s, 2)
        dst = 1 - src

        def colour_step(c, carry2):
            for r in range(2):
                a = r * COLOURS + c
                rows = slice(r * BLK, r * BLK + rows_p)
                low = tall(maps[a, 1], n_p)
                high = tall(maps[a, 2], n_p)
                for z in range(nz):
                    cur = packed[src, a, z, mid, :]
                    new = stay * cur
                    new = new + coef[0, z, rows, :] * packed[src, a, z, PAD - 1 : PAD - 1 + rows_p, :]
                    new = new + coef[1, z, rows, :] * packed[src, a, z, PAD + 1 : PAD + 1 + rows_p, :]
                    new = new + coef[2, z, rows, :] * (pltpu.roll(cur, 1, axis=1) * low)
                    new = new + coef[3, z, rows, :] * (pltpu.roll(cur, ey - 1, axis=1) * high)
                    if z > 0:
                        new = new + coef[4, z, rows, :] * packed[src, a, z - 1, mid, :]
                    if z < nz - 1:
                        new = new + coef[5, z, rows, :] * packed[src, a, z + 1, mid, :]
                    packed[dst, a, z, mid, :] = new
            return carry2

        lax.fori_loop(0, COLOURS, colour_step, 0)
        for z in range(nz):
            cur = spanning[src, z, mid_s, :]
            new = stay * cur
            new = new + coef[0, z] * spanning[src, z, PAD - 1 : PAD - 1 + ex, :]
            new = new + coef[1, z] * spanning[src, z, PAD + 1 : PAD + 1 + ex, :]
            new = new + coef[2, z] * jnp.where(lane_s > 0, pltpu.roll(cur, 1, axis=1), 0.0)
            new = new + coef[3, z] * jnp.where(lane_s < ey - 1, pltpu.roll(cur, ey - 1, axis=1), 0.0)
            if z > 0:
                new = new + coef[4, z] * spanning[src, z - 1, mid_s, :]
            if z < nz - 1:
                new = new + coef[5, z] * spanning[src, z + 1, mid_s, :]
            spanning[dst, z, mid_s, :] = new * span_map[...]
        return carry

    width = 2 * m
    for turn in range(ITERS):
        lax.fori_loop(0, SWEEPS, sweep, 0)
        end = SWEEPS % 2
        strips = [jnp.zeros((ex, ey), jnp.float32) for _ in range(2)]
        for z in range(nz):
            sums = []
            for r in range(2):
                value = packed[end, r * COLOURS, z, mid, :]
                for c in range(1, COLOURS):
                    value = value + packed[end, r * COLOURS + c, z, mid, :]
                sums.append(value)
            gap = jnp.zeros((ex - rows_p, ey), jnp.float32)
            value = (
                spanning[end, z, mid_s, :]
                + jnp.concatenate([sums[0], gap], axis=0)
                + jnp.concatenate([gap, sums[1]], axis=0)
            )
            part[turn, z] = value
            for side in range(2):
                first_lane = 0 if side == 0 else ey - width
                moved = pltpu.roll(value, (width * z - first_lane) % ey, axis=1)
                strips[side] = jnp.where(lane_s // width == z, moved, strips[side])
        for side in range(2):
            part_strip[turn, side] = strips[side]
        send(turn + 1)
        receive(turn + 1)
        from_right = part_y[turn, 0] + part_d[turn, 0]
        from_left = part_y[turn, 1] + part_d[turn, 1]
        final = turn == ITERS - 1
        for z in range(nz):
            left = pltpu.roll(from_left, (-width * z) % ey, axis=1)
            right = pltpu.roll(from_right, (ey - width - width * z) % ey, axis=1)
            total = part[turn, z] + part_x[turn, z]
            total = total + jnp.where(lane_s < width, left, jnp.where(lane_s >= ey - width, right, 0.0))
            scale = 1.0 / jnp.maximum(total, 0.01)
            for r in range(2):
                rows = slice(r * BLK, r * BLK + rows_p)
                for c in range(COLOURS):
                    a = r * COLOURS + c
                    packed[0, a, z, mid, :] = packed[end, a, z, mid, :] * scale[rows]
            spanning[0, z, mid_s, :] = spanning[end, z, mid_s, :] * scale

    def unpack(z, carry):
        span_tall = tall(span, n_s)
        whole = spanning[0, z, mid_s, :]
        gap = jnp.zeros((ex - rows_p, ey), jnp.float32)
        for k in range(nb):
            c = k % COLOURS
            a = COLOURS + c
            value = jnp.where(tall(maps[a, 0], n_p) == float(k), packed[0, a, z, mid, :], 0.0)
            value = jnp.concatenate([gap, value], axis=0)
            if k < sub_y:
                top = jnp.where(tall(maps[c, 0], n_p) == float(k), packed[0, c, z, mid, :], 0.0)
                value = value + jnp.concatenate([top, gap], axis=0)
                value = value + jnp.where(span_tall == float(k), whole, 0.0)
            start[k, z] = value
        pltpu.make_async_copy(start.at[:, z], out_hbm.at[:, z], out_sem.at[z]).start()
        return carry

    lax.fori_loop(0, nz, unpack, 0)
    for z in range(nz):
        pltpu.make_async_copy(start.at[:, z], out_hbm.at[:, z], out_sem.at[z]).wait()
    for phase in range(ITERS + 1):
        sent(phase)


def solution(mesh):
    n_gx, n_gy = mesh.shape["gx"], mesh.shape["gy"]

    def body(rock_props, block_slot, bases_start):
        nb, nz, ex, ey = bases_start.shape
        n_win = 4 * nz - 1
        full = ex + 2 * PAD
        rows_p = BLK + 2 * MARGIN + 2 * PAD
        f32 = jnp.float32
        tx = block_slot.shape[0]
        return pl.pallas_call(
            functools.partial(kernel, n_gx, n_gy),
            out_shape=jax.ShapeDtypeStruct(bases_start.shape, f32),
            in_specs=[
                pl.BlockSpec(memory_space=pl.ANY),
                pl.BlockSpec(memory_space=pltpu.VMEM),
                pl.BlockSpec(memory_space=pl.ANY),
            ],
            out_specs=pl.BlockSpec(memory_space=pl.ANY),
            scratch_shapes=[
                pltpu.VMEM(rock_props.shape, f32),
                pltpu.VMEM(bases_start.shape, f32),
                pltpu.VMEM((n_win, full, ey), f32),
                pltpu.VMEM((n_win, full, ey), f32),
                pltpu.VMEM((2, 2, tx, ey), f32),
                pltpu.VMEM((2, 2, full, ey), f32),
                pltpu.VMEM((6, nz, ex, ey), f32),
                pltpu.VMEM((2 * COLOURS, 3, PAD, ey), f32),
                pltpu.VMEM((ex, ey), f32),
                pltpu.VMEM((2, 2 * COLOURS, nz, rows_p, ey), f32),
                pltpu.VMEM((2, nz, full, ey), f32),
                pltpu.VMEM((ITERS, nz, ex, ey), f32),
                pltpu.VMEM((ITERS, 2, ex, ey), f32),
                pltpu.VMEM((ITERS, nz, ex, ey), f32),
                pltpu.VMEM((ITERS, 2, ex, ey), f32),
                pltpu.VMEM((ITERS, 2, ex, ey), f32),
                pltpu.SemaphoreType.DMA,
                pltpu.SemaphoreType.DMA,
                pltpu.SemaphoreType.DMA((nz,)),
                pltpu.SemaphoreType.DMA((ITERS + 1, 2 * len(DIRS))),
                pltpu.SemaphoreType.DMA((ITERS + 1, 2 * len(DIRS))),
            ],
            compiler_params=pltpu.CompilerParams(collective_id=0, has_side_effects=True),
        )(rock_props, block_slot, bases_start)

    placed = (P(None, None, "gx", "gy"), P("gx", "gy"), P(None, None, "gx", "gy"))
    return jax.shard_map(
        body, mesh=mesh, in_specs=placed, out_specs=P(None, None, "gx", "gy"), check_vma=False
    )
```

time: 134 us -> 38.4 us (0.29)
  the two profiles are of different devices: /device:TPU:11 before, /device:TPU:0 now
where the time goes in v1:
time: 38.4 us; the launch traced here: 38.2 us
  Pallas kernels  35.4 us (92%)
  local copies, waits for them, and re-layouts  2.73 us (7%)
    pallas_call x1, Pallas kernels, body(): pl.pallas_call(functools.partial(kernel, n_gx, n_gy), out_shape=jax.Shape...  35.4 us
    unnamed x1, local copies, waits for them, and re-layouts  2.73 us

profile of v1, /device:TPU:0, one launch (start us, length us, event | category | flops | bytes accessed | tf_op | source)
XLA Modules:
  0.0 38.2 jit_solution(5297394096958295904)
XLA Ops:
  0.0 35.4 %shard_map.37 = f32[12,4,64,128]{3,2,1,0:T(8,128)} custom-call(f32[4,4,32,96]{3,2,1,0:T(8,128)} %rock_hbm.1, s32[32,96]{1,0:T(8,128)} %slot_ref.1, f32[12,4,64,128]{3,2,1,0:T(8,128)} %start_hbm.1), custom_call_target="tpu_custom_call" | custom-call | tf_op jit(solution)/shard_map/pallas_call | solution.py:418
  35.4 2.7 %copy.5 = f32[12,4,64,128]{3,2,1,0:T(8,128)} copy(f32[12,4,64,128]{3,2,1,0:T(8,128)} %shard_map.37) | data formatting | bytes 3145728

commit v2 on v1

--- a/solution.py
+++ b/solution.py
@@ -29,10 +29,10 @@
 
 def kernel(
     n_gx, n_gy,
-    rock_hbm, slot_ref, start_hbm, out_hbm,
-    rock, start, window, joined, strip_out, strip_in, coef, maps, span_map, packed, spanning,
+    rock_hbm, slot_ref, start_hbm, packed_a, spanning_a, held_out, span_out,
+    rock, start, window, joined, strip_out, strip_in, coef, coef_y, same, span_map, packed_b, spanning_b,
     part, part_strip, part_x, part_y, part_d,
-    rock_sem, start_sem, out_sem, send_sem, recv_sem,
+    rock_sem, start_sem, send_sem, recv_sem,
 ):
     m = MARGIN
     nb, nz, ex, ey = start.shape
@@ -167,12 +167,12 @@
         for block in range(2):
             packed_strip = jnp.zeros((tx, ey), jnp.float32)
             for i in range(block * per, min(n_win, block * per + per)):
-                j = i - block * per
+                j = (i - block * per - (1 - side)) % per
                 moved = pltpu.roll(window[i, own_rows, :], (m * j - first) % ey, axis=1)
                 packed_strip = jnp.where(lane_t // m == j, moved, packed_strip)
             if block == 1:
                 for z in range(nz):
-                    spot = m * (per - 1) + z
+                    spot = m * (per - 2 + side) + z
                     moved = pltpu.roll(window[KY + z, own_rows, :], (spot - extra) % ey, axis=1)
                     packed_strip = jnp.where(lane_t == spot, moved, packed_strip)
             strip_out[side, block] = packed_strip
@@ -204,12 +204,13 @@
                 fits = jnp.logical_and(value >= 0.0, jnp.logical_and(colour == float(c), value != span))
                 held = jnp.where(fits, value, held)
             a = r * COLOURS + c
-            maps[a, 0] = held
+            held_out[a] = held
             taken = held >= 0.0
             low = jnp.logical_and(taken, jnp.logical_and(lane > 0, pltpu.roll(held, 1, axis=1) == held))
             high = jnp.logical_and(taken, jnp.logical_and(lane < ey - 1, pltpu.roll(held, ey - 1, axis=1) == held))
-            maps[a, 1] = jnp.where(low, 1.0, 0.0)
-            maps[a, 2] = jnp.where(high, 1.0, 0.0)
+            same[a, 0] = jnp.where(low, 1.0, 0.0)
+            same[a, 1] = jnp.where(high, 1.0, 0.0)
+    span_out[...] = span
     both = jnp.maximum(reach[0], reach[1])
     span_map[...] = jnp.concatenate(
         [tall(reach[0], BLK // PAD), tall(both, (ex - 2 * BLK) // PAD), tall(reach[1], BLK // PAD)], axis=0
@@ -224,10 +225,12 @@
     inside = inside * jnp.where(col < m, edge(gy == 0), 1.0)
     inside = inside * jnp.where(col >= m + ty, edge(gy == n_gy - 1), 1.0)
 
-    packed[:, :, :, :PAD, :] = jnp.zeros(packed.shape[:3] + (PAD, ey), jnp.float32)
-    packed[:, :, :, PAD + rows_p :, :] = jnp.zeros(packed.shape[:3] + (PAD, ey), jnp.float32)
-    spanning[:, :, :PAD, :] = jnp.zeros(spanning.shape[:2] + (PAD, ey), jnp.float32)
-    spanning[:, :, PAD + ex :, :] = jnp.zeros(spanning.shape[:2] + (PAD, ey), jnp.float32)
+    for ref in (packed_a, packed_b):
+        ref[:, :, :PAD, :] = jnp.zeros(ref.shape[:2] + (PAD, ey), jnp.float32)
+        ref[:, :, PAD + rows_p :, :] = jnp.zeros(ref.shape[:2] + (PAD, ey), jnp.float32)
+    for ref in (spanning_a, spanning_b):
+        ref[:, :PAD, :] = jnp.zeros((nz, PAD, ey), jnp.float32)
+        ref[:, PAD + ex :, :] = jnp.zeros((nz, PAD, ey), jnp.float32)
     mid = slice(PAD, PAD + rows_p)
     mid_s = slice(PAD, PAD + ex)
     n_p = rows_p // PAD
@@ -240,14 +243,14 @@
             slot_count = sub_y if r == 0 else nb
             for c in range(COLOURS):
                 a = r * COLOURS + c
-                held = maps[a, 0]
+                held = held_out[a]
                 own = jnp.where(held == slot_rows[r], 1.0, 0.0)
                 none = jnp.zeros((m, ey), jnp.float32)
                 value = jnp.concatenate([none, tall(own, BLK // PAD), none], axis=0)
                 held_tall = tall(held, n_p)
                 for k in range(c, slot_count, COLOURS):
                     value = value + jnp.where(held_tall == float(k), start[k, z, rows, :], 0.0)
-                packed[0, a, z, mid, :] = value * inside[rows]
+                packed_a[a, z, mid, :] = value * inside[rows]
         none = jnp.zeros((m, ey), jnp.float32)
         value = jnp.concatenate(
             [none]
@@ -258,18 +261,19 @@
         span_tall = tall(span, n_s)
         for k in range(sub_y):
             value = value + jnp.where(span_tall == float(k), start[k, z], 0.0)
-        spanning[0, z, mid_s, :] = value * inside * span_map[...]
+        spanning_a[z, mid_s, :] = value * inside * span_map[...]
         return carry
 
     lax.fori_loop(0, nz, fill, 0)
 
     receive(0)
     lane_f = lax.broadcasted_iota(jnp.int32, (full, ey), 1)
+    border = jnp.logical_or(lane_f < m, lane_f >= ey - m)
     for i in range(n_win):
         block, j = i // per, i % per
-        left = pltpu.roll(strip_in[1, block], (-m * j) % ey, axis=1)
-        right = pltpu.roll(strip_in[0, block], (ey - m - m * j) % ey, axis=1)
-        joined[i] = jnp.where(lane_f < m, left, jnp.where(lane_f >= ey - m, right, window[i]))
+        near = jnp.where(lane_f // m == j, strip_in[1, block], strip_in[0, block])
+        near = pltpu.roll(near, (-m * j) % ey, axis=1)
+        joined[i] = jnp.where(border, near, window[i])
     lane_s = lax.broadcasted_iota(jnp.int32, (ex, ey), 1)
     for z in range(nz):
         here = joined[KX + z, mid_s, :]
@@ -279,6 +283,7 @@
         spot = m * (per - 1) + z
         outer = pltpu.roll(strip_in[1, 1, mid_s, :], (-spot) % ey, axis=1)
         link_yl = harmonic(jnp.where(lane_s == 0, outer, pltpu.roll(here, 1, axis=1)), here)
+        spot = m * (per - 2) + z
         outer = pltpu.roll(strip_in[0, 1, mid_s, :], (ey - 1 - spot) % ey, axis=1)
         link_yh = harmonic(here, jnp.where(lane_s == ey - 1, outer, pltpu.roll(here, ey - 1, axis=1)))
         links = [link_xl, link_xh, link_yl, link_yh]
@@ -293,116 +298,138 @@
         for link in links[1:]:
             total = total + link
         diagonal = jnp.maximum(total + 0.05 * joined[ST + z, mid_s, :], 0.01)
-        factor = WEIGHT / diagonal
+        factor = (WEIGHT / (1.0 - WEIGHT)) / diagonal
         for place_no, link in zip(places, links):
-            coef[place_no, z] = link * factor
-
-    stay = 1.0 - WEIGHT
-
-    def sweep(s, carry):
-        src = lax.rem(s, 2)
-        dst = 1 - src
-
-        def colour_step(c, carry2):
+            value = link * factor
+            if place_no == 2:
+                value = jnp.where(lane_s > 0, value, 0.0)
+            if place_no == 3:
+                value = jnp.where(lane_s < ey - 1, value, 0.0)
+            coef[place_no, z] = value
+            if place_no in (2, 3):
+                for a in range(2 * COLOURS):
+                    first_row = (a // COLOURS) * BLK
+                    coef_y[a, place_no - 2, z] = value[first_row : first_row + rows_p] * tall(
+                        same[a, place_no - 2], n_p
+                    )
+
+    chunk = rows_p // 2
+
+    def sweep(src, dst, src_s, dst_s):
+        def chunk_step(t, carry):
+            top = pl.multiple_of(t * chunk, PAD)
+            rows_c = pl.ds(top, chunk)
+            rows_m = pl.ds(top + PAD, chunk)
             for r in range(2):
-                a = r * COLOURS + c
-                rows = slice(r * BLK, r * BLK + rows_p)
-                low = tall(maps[a, 1], n_p)
-                high = tall(maps[a, 2], n_p)
+                rows = pl.ds(top + r * BLK, chunk)
                 for z in range(nz):
-                    cur = packed[src, a, z, mid, :]
-                    new = stay * cur
-                    new = new + coef[0, z, rows, :] * packed[src, a, z, PAD - 1 : PAD - 1 + rows_p, :]
-                    new = new + coef[1, z, rows, :] * packed[src, a, z, PAD + 1 : PAD + 1 + rows_p, :]
-                    new = new + coef[2, z, rows, :] * (pltpu.roll(cur, 1, axis=1) * low)
-                    new = new + coef[3, z, rows, :] * (pltpu.roll(cur, ey - 1, axis=1) * high)
-                    if z > 0:
-                        new = new + coef[4, z, rows, :] * packed[src, a, z - 1, mid, :]
-                    if z < nz - 1:
-                        new = new + coef[5, z, rows, :] * packed[src, a, z + 1, mid, :]
-                    packed[dst, a, z, mid, :] = new
-            return carry2
-
-        lax.fori_loop(0, COLOURS, colour_step, 0)
+                    xl, xh = coef[0, z, rows, :], coef[1, z, rows, :]
+                    for c in range(COLOURS):
+                        a = r * COLOURS + c
+                        cur = src[a, z, rows_m, :]
+                        new = cur + xl * src[a, z, pl.ds(top + PAD - 1, chunk), :]
+                        new = new + xh * src[a, z, pl.ds(top + PAD + 1, chunk), :]
+                        if z > 0:
+                            new = new + coef[4, z, rows, :] * src[a, z - 1, rows_m, :]
+                        if z < nz - 1:
+                            new = new + coef[5, z, rows, :] * src[a, z + 1, rows_m, :]
+                        new = new + coef_y[a, 0, z, rows_c, :] * pltpu.roll(cur, 1, axis=1)
+                        new = new + coef_y[a, 1, z, rows_c, :] * pltpu.roll(cur, ey - 1, axis=1)
+                        dst[a, z, rows_m, :] = new
+            return carry
+
+        lax.fori_loop(0, 2, chunk_step, 0)
         for z in range(nz):
-            cur = spanning[src, z, mid_s, :]
-            new = stay * cur
-            new = new + coef[0, z] * spanning[src, z, PAD - 1 : PAD - 1 + ex, :]
-            new = new + coef[1, z] * spanning[src, z, PAD + 1 : PAD + 1 + ex, :]
-            new = new + coef[2, z] * jnp.where(lane_s > 0, pltpu.roll(cur, 1, axis=1), 0.0)
-            new = new + coef[3, z] * jnp.where(lane_s < ey - 1, pltpu.roll(cur, ey - 1, axis=1), 0.0)
+            cur = src_s[z, mid_s, :]
+            new = cur + coef[0, z] * src_s[z, PAD - 1 : PAD - 1 + ex, :]
+            new = new + coef[1, z] * src_s[z, PAD + 1 : PAD + 1 + ex, :]
             if z > 0:
-                new = new + coef[4, z] * spanning[src, z - 1, mid_s, :]
+                new = new + coef[4, z] * src_s[z - 1, mid_s, :]
             if z < nz - 1:
-                new = new + coef[5, z] * spanning[src, z + 1, mid_s, :]
-            spanning[dst, z, mid_s, :] = new * span_map[...]
-        return carry
-
+                new = new + coef[5, z] * src_s[z + 1, mid_s, :]
+            new = new + coef[2, z] * pltpu.roll(cur, 1, axis=1)
+            new = new + coef[3, z] * pltpu.roll(cur, ey - 1, axis=1)
+            dst_s[z, mid_s, :] = new * span_map[...]
+
+    unscale = (1.0 - WEIGHT) ** SWEEPS
     width = 2 * m
     for turn in range(ITERS):
-        lax.fori_loop(0, SWEEPS, sweep, 0)
-        end = SWEEPS % 2
+        here, there = (packed_a, spanning_a), (packed_b, spanning_b)
+        for _ in range(SWEEPS):
+            sweep(here[0], there[0], here[1], there[1])
+            here, there = there, here
+        packed, spanning = here
         strips = [jnp.zeros((ex, ey), jnp.float32) for _ in range(2)]
         for z in range(nz):
             sums = []
             for r in range(2):
-                value = packed[end, r * COLOURS, z, mid, :]
+                value = packed[r * COLOURS, z, mid, :]
                 for c in range(1, COLOURS):
-                    value = value + packed[end, r * COLOURS + c, z, mid, :]
+                    value = value + packed[r * COLOURS + c, z, mid, :]
                 sums.append(value)
             gap = jnp.zeros((ex - rows_p, ey), jnp.float32)
             value = (
-                spanning[end, z, mid_s, :]
+                spanning[z, mid_s, :]
                 + jnp.concatenate([sums[0], gap], axis=0)
                 + jnp.concatenate([gap, sums[1]], axis=0)
             )
+            value = value * unscale
             part[turn, z] = value
             for side in range(2):
                 first_lane = 0 if side == 0 else ey - width
-                moved = pltpu.roll(value, (width * z - first_lane) % ey, axis=1)
-                strips[side] = jnp.where(lane_s // width == z, moved, strips[side])
+                spot = (z - (1 - side)) % nz
+                moved = pltpu.roll(value, (width * spot - first_lane) % ey, axis=1)
+                strips[side] = jnp.where(lane_s // width == spot, moved, strips[side])
         for side in range(2):
             part_strip[turn, side] = strips[side]
         send(turn + 1)
         receive(turn + 1)
         from_right = part_y[turn, 0] + part_d[turn, 0]
         from_left = part_y[turn, 1] + part_d[turn, 1]
-        final = turn == ITERS - 1
         for z in range(nz):
-            left = pltpu.roll(from_left, (-width * z) % ey, axis=1)
-            right = pltpu.roll(from_right, (ey - width - width * z) % ey, axis=1)
+            near = jnp.where(lane_s // width == z, from_left, from_right)
+            near = pltpu.roll(near, (-width * z) % ey, axis=1)
             total = part[turn, z] + part_x[turn, z]
-            total = total + jnp.where(lane_s < width, left, jnp.where(lane_s >= ey - width, right, 0.0))
-            scale = 1.0 / jnp.maximum(total, 0.01)
+            total = total + jnp.where(jnp.logical_or(lane_s < width, lane_s >= ey - width), near, 0.0)
+            scale = unscale / jnp.maximum(total, 0.01)
             for r in range(2):
                 rows = slice(r * BLK, r * BLK + rows_p)
                 for c in range(COLOURS):
                     a = r * COLOURS + c
-                    packed[0, a, z, mid, :] = packed[end, a, z, mid, :] * scale[rows]
-            spanning[0, z, mid_s, :] = spanning[end, z, mid_s, :] * scale
-
-    def unpack(z, carry):
-        span_tall = tall(span, n_s)
-        whole = spanning[0, z, mid_s, :]
-        gap = jnp.zeros((ex - rows_p, ey), jnp.float32)
+                    packed_a[a, z, mid, :] = packed[a, z, mid, :] * scale[rows]
+            spanning_a[z, mid_s, :] = spanning[z, mid_s, :] * scale
+
+    for phase in range(ITERS + 1):
+        sent(phase)
+
+
+def unpack(packed, spanning, held, span_ref, out_hbm, out, out_sem):
+    nb, nz, ex, ey = out.shape
+    rows_p = packed.shape[2] - 2 * PAD
+    n_p, n_s = rows_p // PAD, ex // PAD
+    mid, mid_s = slice(PAD, PAD + rows_p), slice(PAD, PAD + ex)
+    gap = jnp.zeros((ex - rows_p, ey), jnp.float32)
+    in_top = nb // 2
+
+    def layer(z, carry):
+        span_tall = tall(span_ref[...], n_s)
+        whole = spanning[z, mid_s, :]
         for k in range(nb):
             c = k % COLOURS
             a = COLOURS + c
-            value = jnp.where(tall(maps[a, 0], n_p) == float(k), packed[0, a, z, mid, :], 0.0)
+            value = jnp.where(tall(held[a], n_p) == float(k), packed[a, z, mid, :], 0.0)
             value = jnp.concatenate([gap, value], axis=0)
-            if k < sub_y:
-                top = jnp.where(tall(maps[c, 0], n_p) == float(k), packed[0, c, z, mid, :], 0.0)
+            if k < in_top:
+                top = jnp.where(tall(held[c], n_p) == float(k), packed[c, z, mid, :], 0.0)
                 value = value + jnp.concatenate([top, gap], axis=0)
                 value = value + jnp.where(span_tall == float(k), whole, 0.0)
-            start[k, z] = value
-        pltpu.make_async_copy(start.at[:, z], out_hbm.at[:, z], out_sem.at[z]).start()
+            out[k, z] = value
+        pltpu.make_async_copy(out.at[:, z], out_hbm.at[:, z], out_sem.at[z]).start()
         return carry
 
-    lax.fori_loop(0, nz, unpack, 0)
+    lax.fori_loop(0, nz, layer, 0)
     for z in range(nz):
-        pltpu.make_async_copy(start.at[:, z], out_hbm.at[:, z], out_sem.at[z]).wait()
-    for phase in range(ITERS + 1):
-        sent(phase)
+        pltpu.make_async_copy(out.at[:, z], out_hbm.at[:, z], out_sem.at[z]).wait()
 
 
 def solution(mesh):
@@ -412,18 +439,22 @@
         nb, nz, ex, ey = bases_start.shape
         n_win = 4 * nz - 1
         full = ex + 2 * PAD
-        rows_p = BLK + 2 * MARGIN + 2 * PAD
+        rows_p = BLK + 2 * MARGIN
         f32 = jnp.float32
         tx = block_slot.shape[0]
-        return pl.pallas_call(
+        vmem = pl.BlockSpec(memory_space=pltpu.VMEM)
+        anywhere = pl.BlockSpec(memory_space=pl.ANY)
+        packed_shape = (2 * COLOURS, nz, rows_p + 2 * PAD, ey)
+        held = pl.pallas_call(
             functools.partial(kernel, n_gx, n_gy),
-            out_shape=jax.ShapeDtypeStruct(bases_start.shape, f32),
-            in_specs=[
-                pl.BlockSpec(memory_space=pl.ANY),
-                pl.BlockSpec(memory_space=pltpu.VMEM),
-                pl.BlockSpec(memory_space=pl.ANY),
-            ],
-            out_specs=pl.BlockSpec(memory_space=pl.ANY),
+            out_shape=(
+                jax.ShapeDtypeStruct(packed_shape, f32),
+                jax.ShapeDtypeStruct((nz, full, ey), f32),
+                jax.ShapeDtypeStruct((2 * COLOURS, PAD, ey), f32),
+                jax.ShapeDtypeStruct((PAD, ey), f32),
+            ),
+            in_specs=[anywhere, vmem, anywhere],
+            out_specs=(vmem,) * 4,
             scratch_shapes=[
                 pltpu.VMEM(rock_props.shape, f32),
                 pltpu.VMEM(bases_start.shape, f32),
@@ -432,10 +463,11 @@
                 pltpu.VMEM((2, 2, tx, ey), f32),
                 pltpu.VMEM((2, 2, full, ey), f32),
                 pltpu.VMEM((6, nz, ex, ey), f32),
-                pltpu.VMEM((2 * COLOURS, 3, PAD, ey), f32),
+                pltpu.VMEM((2 * COLOURS, 2, nz, rows_p, ey), f32),
+                pltpu.VMEM((2 * COLOURS, 2, PAD, ey), f32),
                 pltpu.VMEM((ex, ey), f32),
-                pltpu.VMEM((2, 2 * COLOURS, nz, rows_p, ey), f32),
-                pltpu.VMEM((2, nz, full, ey), f32),
+                pltpu.VMEM(packed_shape, f32),
+                pltpu.VMEM((nz, full, ey), f32),
                 pltpu.VMEM((ITERS, nz, ex, ey), f32),
                 pltpu.VMEM((ITERS, 2, ex, ey), f32),
                 pltpu.VMEM((ITERS, nz, ex, ey), f32),
@@ -443,12 +475,18 @@
                 pltpu.VMEM((ITERS, 2, ex, ey), f32),
                 pltpu.SemaphoreType.DMA,
                 pltpu.SemaphoreType.DMA,
-                pltpu.SemaphoreType.DMA((nz,)),
                 pltpu.SemaphoreType.DMA((ITERS + 1, 2 * len(DIRS))),
                 pltpu.SemaphoreType.DMA((ITERS + 1, 2 * len(DIRS))),
             ],
             compiler_params=pltpu.CompilerParams(collective_id=0, has_side_effects=True),
         )(rock_props, block_slot, bases_start)
+        return pl.pallas_call(
+            unpack,
+            out_shape=jax.ShapeDtypeStruct(bases_start.shape, f32),
+            in_specs=[vmem] * 4,
+            out_specs=anywhere,
+            scratch_shapes=[pltpu.VMEM(bases_start.shape, f32), pltpu.SemaphoreType.DMA((nz,))],
+        )(*held)
 
     placed = (P(None, None, "gx", "gy"), P("gx", "gy"), P(None, None, "gx", "gy"))
     return jax.shard_map(

time: 38.4 us -> 27.8 us (0.72)
  Pallas kernels: 35.4 us -> 27.6 us
  local copies, waits for them, and re-layouts: 2.73 us -> 0 us
    pallas_call x1 -> x2, Pallas kernels: 35.4 us -> 27.6 us  [the longest x1 25.1 us: body(): pl.pallas_call(functools.partial(kernel, n_gx, n_gy), out_shape=(jax.Shap...]
    unnamed x1 -> x0, local copies, waits for them, and re-layouts: 2.73 us -> none
where the time goes in v2:
time: 27.8 us; the launch traced here: 27.6 us
  Pallas kernels  27.6 us (99%)
    pallas_call x1, Pallas kernels, body(): pl.pallas_call(functools.partial(kernel, n_gx, n_gy), out_shape=(jax.Shap...  25.1 us
    pallas_call x1, Pallas kernels, body(): pl.pallas_call(unpack, out_shape=jax.ShapeDtypeStruct(bases_start.shape,...  2.44 us

profile of v2, /device:TPU:0, one launch (start us, length us, event | category | flops | bytes accessed | tf_op | source)
XLA Modules:
  0.0 27.6 jit_solution(11177578530820558781)
XLA Ops:
  0.0 25.1 %shard_map.37 = (f32[6,4,64,128]{3,2,1,0:T(8,128)}, f32[4,80,128]{2,1,0:T(8,128)}, f32[6,8,128]{2,1,0:T(8,128)}, f32[8,128]{1,0:T(8,128)}) custom-call(f32[4,4,32,96]{3,2,1,0:T(8,128)} %rock_hbm.1, s32[32,96]{1,0:T(8,128)} %slot_ref.1, f32[12,4,64,128]{3,2,1,0:T(8,128)} %start_hbm.1), custom_call_target="tpu_custom_call" | custom-call | tf_op jit(solution)/shard_map/pallas_call | solution.py:448
  25.1 2.4 %shard_map.38 = f32[12,4,64,128]{3,2,1,0:T(8,128)} custom-call(f32[6,4,64,128]{3,2,1,0:T(8,128)} %get-tuple-element.9.packed, f32[4,80,128]{2,1,0:T(8,128)} %get-tuple-element.10.spanning, f32[6,8,128]{2,1,0:T(8,128)} %get-tuple-element.11.held, f32[8,128]{1,0:T(8,128)} %get-tuple-element.12.span_ref), custom_call_target="tpu_custom_call" | custom-call | tf_op jit(solution)/shard_map/pallas_call | solution.py:483

commit v3 on v2

--- a/solution.py
+++ b/solution.py
@@ -101,8 +101,8 @@
     def sum_messages(turn, dx, dy):
         if dy == 0:
             if dx < 0:
-                return [(part.at[turn, :, pl.ds(0, half)], part_x.at[turn, :, pl.ds(half, half)])]
-            return [(part.at[turn, :, pl.ds(half, half)], part_x.at[turn, :, pl.ds(0, half)])]
+                return [(part.at[turn, z, pl.ds(0, half)], part_x.at[turn, z, pl.ds(half, half)]) for z in range(nz)]
+            return [(part.at[turn, z, pl.ds(half, half)], part_x.at[turn, z, pl.ds(0, half)]) for z in range(nz)]
         side = 0 if dy < 0 else 1
         if dx == 0:
             return [(part_strip.at[turn, side], part_y.at[turn, side])]
@@ -110,9 +110,9 @@
             return [(part_strip.at[turn, side, pl.ds(0, half)], part_d.at[turn, side, pl.ds(half, half)])]
         return [(part_strip.at[turn, side, pl.ds(half, half)], part_d.at[turn, side, pl.ds(0, half)])]
 
-    def copies(phase, dx, dy):
+    def copies(phase, dx, dy, layer=None):
         messages = rock_messages(dx, dy) if phase == 0 else sum_messages(phase - 1, dx, dy)
-        base = 2 * DIRS.index((dx, dy))
+        base = max(2, nz) * DIRS.index((dx, dy))
         return [
             pltpu.make_async_remote_copy(
                 src_ref=src,
@@ -123,13 +123,17 @@
                 device_id_type=MESH,
             )
             for i, (src, dst) in enumerate(messages)
+            if layer is None or i == layer
         ]
 
-    def send(phase):
+    def send(phase, along_x, layer=None):
         for dx, dy in DIRS:
+            if (dy == 0) != along_x:
+                continue
+
             @pl.when(exists(dx, dy))
             def _(dx=dx, dy=dy):
-                for copy in copies(phase, dx, dy):
+                for copy in copies(phase, dx, dy, layer):
                     copy.start()
 
     def receive(phase):
@@ -160,6 +164,8 @@
         place(ST + z, rock[3, z])
         if z < nz - 1:
             place(TZ + z, harmonic(rock[2, z], rock[2, z + 1]))
+    pl.semaphore_wait(barrier, expected)
+    send(0, True)
     per = LANES // m
     for side in range(2):
         first = m if side == 0 else m + ty - m
@@ -177,8 +183,7 @@
                     packed_strip = jnp.where(lane_t == spot, moved, packed_strip)
             strip_out[side, block] = packed_strip
 
-    pl.semaphore_wait(barrier, expected)
-    send(0)
+    send(0, False)
 
     lane = lax.broadcasted_iota(jnp.int32, (PAD, ey), 1)
     slot_rows = []
@@ -375,6 +380,7 @@
             )
             value = value * unscale
             part[turn, z] = value
+            send(turn + 1, True, z)
             for side in range(2):
                 first_lane = 0 if side == 0 else ey - width
                 spot = (z - (1 - side)) % nz
@@ -382,7 +388,7 @@
                 strips[side] = jnp.where(lane_s // width == spot, moved, strips[side])
         for side in range(2):
             part_strip[turn, side] = strips[side]
-        send(turn + 1)
+        send(turn + 1, False)
         receive(turn + 1)
         from_right = part_y[turn, 0] + part_d[turn, 0]
         from_left = part_y[turn, 1] + part_d[turn, 1]
@@ -448,10 +454,10 @@
         held = pl.pallas_call(
             functools.partial(kernel, n_gx, n_gy),
             out_shape=(
-                jax.ShapeDtypeStruct(packed_shape, f32),
-                jax.ShapeDtypeStruct((nz, full, ey), f32),
-                jax.ShapeDtypeStruct((2 * COLOURS, PAD, ey), f32),
-                jax.ShapeDtypeStruct((PAD, ey), f32),
+                pltpu.VMEM(packed_shape, f32),
+                pltpu.VMEM((nz, full, ey), f32),
+                pltpu.VMEM((2 * COLOURS, PAD, ey), f32),
+                pltpu.VMEM((PAD, ey), f32),
             ),
             in_specs=[anywhere, vmem, anywhere],
             out_specs=(vmem,) * 4,
@@ -475,8 +481,8 @@
                 pltpu.VMEM((ITERS, 2, ex, ey), f32),
                 pltpu.SemaphoreType.DMA,
                 pltpu.SemaphoreType.DMA,
-                pltpu.SemaphoreType.DMA((ITERS + 1, 2 * len(DIRS))),
-                pltpu.SemaphoreType.DMA((ITERS + 1, 2 * len(DIRS))),
+                pltpu.SemaphoreType.DMA((ITERS + 1, max(2, nz) * len(DIRS))),
+                pltpu.SemaphoreType.DMA((ITERS + 1, max(2, nz) * len(DIRS))),
             ],
             compiler_params=pltpu.CompilerParams(collective_id=0, has_side_effects=True),
         )(rock_props, block_slot, bases_start)
@@ -486,7 +492,7 @@
             in_specs=[vmem] * 4,
             out_specs=anywhere,
             scratch_shapes=[pltpu.VMEM(bases_start.shape, f32), pltpu.SemaphoreType.DMA((nz,))],
-        )(*held)
+        )(*(pltpu.with_memory_space_constraint(value, pltpu.VMEM) for value in held))
 
     placed = (P(None, None, "gx", "gy"), P("gx", "gy"), P(None, None, "gx", "gy"))
     return jax.shard_map(

time: 27.8 us -> 27 us (0.971)
  Pallas kernels: 27.6 us -> 26.6 us
    pallas_call x1, Pallas kernels: 2.44 us -> 1.21 us  [body(): pl.pallas_call(unpack, out_shape=jax.ShapeDtypeStruct(bases_start.shape,...]
    pallas_call x1, Pallas kernels: 25.1 us -> 25.4 us  [body(): pl.pallas_call(functools.partial(kernel, n_gx, n_gy), out_shape=(pltpu.VM...]
where the time goes in v3:
time: 27 us; the launch traced here: 26.7 us
  Pallas kernels  26.6 us (99%)
    pallas_call x1, Pallas kernels, body(): pl.pallas_call(functools.partial(kernel, n_gx, n_gy), out_shape=(pltpu.VM...  25.4 us
    pallas_call x1, Pallas kernels, body(): pl.pallas_call(unpack, out_shape=jax.ShapeDtypeStruct(bases_start.shape,...  1.21 us

profile of v3, /device:TPU:0, one launch (start us, length us, event | category | flops | bytes accessed | tf_op | source)
XLA Modules:
  0.0 26.7 jit_solution(2958959090130827100)
XLA Ops:
  0.0 25.4 %shard_map.37 = (f32[6,4,64,128]{3,2,1,0:T(8,128)S(1)}, f32[4,80,128]{2,1,0:T(8,128)S(1)}, f32[6,8,128]{2,1,0:T(8,128)S(1)}, f32[8,128]{1,0:T(8,128)S(1)}) custom-call(f32[4,4,32,96]{3,2,1,0:T(8,128)} %rock_hbm.1, s32[32,96]{1,0:T(8,128)} %slot_ref.1, f32[12,4,64,128]{3,2,1,0:T(8,128)} %start_hbm.1), custom_call_target="tpu_custom_call" | custom-call | tf_op jit(solution)/shard_map/pallas_call | solution.py:454
  25.4 1.2 %shard_map.38 = f32[12,4,64,128]{3,2,1,0:T(8,128)} custom-call(f32[6,4,64,128]{3,2,1,0:T(8,128)S(1)} %get-tuple-element.9.packed, f32[4,80,128]{2,1,0:T(8,128)S(1)} %get-tuple-element.10.spanning, f32[6,8,128]{2,1,0:T(8,128)S(1)} %get-tuple-element.11.held, f32[8,128]{1,0:T(8,128)S(1)} %get-tuple-element.12.span_ref), custom_call_target="tpu_custom_call" | custom-call | tf_op jit(solution)/shard_map/pallas_call | solution.py:489
